TPU v7x, 512 devices: a whole 4x4x16 slice. The times are simulated.
512 devices in a mesh: view: 8 (over y, x_lo), tile: 64 (over x_hi, z, core).
Axes of the slice: x: 4 (x_hi: 2, x_lo: 2; x = x_hi * 2 + x_lo), y: 4, z: 16, core: 2. Of those that a mesh axis runs over, the one named last changes fastest.
Arguments:
- estimate: float32 [128, 2048, 128], P('view', 'tile'), may hold values from 0.5 to 2
- images: float32 [8, 128, 2048, 128], P('view', None, 'tile'), may hold values from 0.2 to 2
- profiles: float32 [8, 3, 15], P('view'), may hold values from 0.02 to 0.15
Outputs:
- updated: float32 [128, 2048, 128], P('view', 'tile')
All inputs are finite; a program needn't handle non-finite values.
Results may differ from a plain program's by a relative error of at most 0.0003.
Values sent between devices are 32-bit elements; how exact they have to be, the bound alone decides.
A program may use at most 64 MiB of HBM per device.

v0:
```python
import jax
import jax.numpy as jnp
from jax import lax
from jax.sharding import PartitionSpec as P


def extended(value, sides, width):
    for axis, dim in sides:
        size, length = (lax.axis_size(axis), value.shape[dim])
        up = [(i, (i + 1) % size) for i in range(size - 1)]
        down = [(j, i) for i, j in up]
        last = lax.slice_in_dim(value, length - width, length, axis=dim)
        first = lax.slice_in_dim(value, 0, width, axis=dim)
        before = lax.ppermute(last, axis, up)
        after = lax.ppermute(first, axis, down)
        value = jnp.concatenate([before, value, after], axis=dim)
    return value


def from_behind(value, axis, by):
    size = lax.axis_size(axis)
    return lax.ppermute(value, axis, [(i, (i + by) % size) for i in range(size)])


def valid_pass(padded, kernel, dimension):
    length = kernel.shape[0]
    extent = padded.shape[dimension] - length + 1
    summed = kernel[0] * lax.slice_in_dim(padded, 0, extent, axis=dimension)
    for offset in range(1, length):
        summed = summed + kernel[offset] * lax.slice_in_dim(
            padded, offset, offset + extent, axis=dimension
        )
    return summed


def correlate(volume, kernel, dimension):
    radius = kernel.shape[0] // 2
    padding = [(0, 0)] * volume.ndim
    padding[dimension] = (radius, radius)
    return valid_pass(jnp.pad(volume, padding), kernel, dimension)


def rim_halo(volume, radius):
    return extended(volume, (("tile", 1),), radius)


def forward_cycle(volume):
    return from_behind(volume, "view", 1)


def update_rims(current, observed, kernel):
    radius = kernel.shape[1] // 2
    partial_blur = correlate(correlate(current, kernel[0], 0), kernel[2], 2)
    blurred = valid_pass(rim_halo(partial_blur, radius), kernel[1], 1)
    quotient = observed / blurred
    backward = valid_pass(rim_halo(quotient, radius), kernel[1][::-1], 1)
    backward = correlate(backward, kernel[2][::-1], 2)
    backward = correlate(backward, kernel[0][::-1], 0)
    return current * backward


def shards(estimate, images, profiles):
    view_count = lax.axis_size("view")
    view_index = lax.axis_index("view")
    kernel = profiles[0]
    depth = estimate.shape[0]
    current = estimate
    for number in range(view_count):
        slab_index = (view_index - number) % view_count
        observed = lax.dynamic_slice_in_dim(images[0], slab_index * depth, depth, 0)
        current = forward_cycle(update_rims(current, observed, kernel))
    return current


def solution(mesh):
    return jax.shard_map(
        shards,
        mesh=mesh,
        in_specs=(P("view", "tile", None), P("view", None, "tile", None), P("view", None, None)),
        out_specs=P("view", "tile", None),
        check_vma=False,
    )
```

profile of v0, /device:TPU:6, one launch (start us, length us, event | category | flops | bytes accessed | tf_op | source)
XLA Modules:
  0.0 754.5 jit_solution(9568375095796426340)
XLA Ops:
  5.1 12.7 %fusion.630 = f32[16,32,128]{2,1,0:T(8,128)S(1)} fusion(f32[16,32,128]{2,1,0:T(8,128)} %param.3, f32[]{:T(128)} %bitcast.19, f32[]{:T(128)} %bitcast.18, f32[]{:T(128)} %bitcast.17, f32[]{:T(128)} %bitcast.16, f32[]{:T(128)} %bitcast.15, f32[]{:T(128)} %bitcast.14, f32[]{:T(128)} %bitcast.13, f32[]{:T(128)} %bitcast.12, f32[]{:T(128)} %bitcast.11, ...), kind=kLoop, calls=%fused_computation.1462 | loop fusion | flops 1900544 | bytes 524348 | tf_op jit(solution)/shard_map/add | solution.py:30
  17.8 10.4 %fusion.1086 = f32[16,32,128]{2,1,0:T(8,128)S(1)} fusion(f32[16,32,128]{2,1,0:T(8,128)S(1)} %fusion.630, f32[]{:T(128)} %bitcast.32, f32[]{:T(128)} %bitcast.31, f32[]{:T(128)} %bitcast.30, f32[]{:T(128)} %bitcast.29, f32[]{:T(128)} %bitcast.28, f32[]{:T(128)} %bitcast.27, f32[]{:T(128)} %bitcast.26, f32[]{:T(128)} %bitcast.25, f32[]{:T(128)} %bitcast.24, ...), kind=kLoop, calls=%fused_computation.1918 | loop fusion | flops 1900544 | bytes 524348 | tf_op jit(solution)/shard_map/add | solution.py:30
  30.2 11.7 %collective-permute-start.1 = (f32[16,7,128]{2,1,0:T(8,128)S(1)}, f32[16,7,128]{2,1,0:T(8,128)S(1)}, u32[]{:S(2)}, u32[]{:S(2)}) collective-permute-start(f32[16,7,128]{2,1,0:T(8,128)S(1)} %get-tuple-element.36), channel_id=1, source_target_pairs={{1,0},{2,1},{3,2},{4,3},{5,4},{6,5},{7,6},{8,7},{9,8},{10,9},{11,1... | collective-permute-start | bytes 172040 | tf_op jit(solution)/shard_map/ppermute | solution.py:15
  43.7 10.8 %fusion.581 = f32[16,32,128]{2,1,0:T(8,128)S(1)} fusion(f32[16,32,128]{2,1,0:T(8,128)S(1)} %fusion.1086, f32[16,7,128]{2,1,0:T(8,128)S(1)} %collective-permute-done.1, f32[16,7,128]{2,1,0:T(8,128)S(1)} %collective-permute-done, f32[1,128,32,128]{3,2,1,0:T(8,128)} %param.4, s32[]{:T(128)S(6)} %select_n.60, f32[]{:T(128)} %bitcast.45, f32[]{:T(128)} %bitcast.44, ...), kind=kLoop, calls=%fused_computation.1413 | loop fusion | flops 2883584 | bytes 901184 | tf_op jit(solution)/shard_map/div | solution.py:55
  75.5 10.4 %fusion.1114 = f32[16,32,128]{2,1,0:T(8,128)S(1)} fusion(f32[16,32,128]{2,1,0:T(8,128)S(1)} %fusion.542, f32[]{:T(128)} %bitcast.32, f32[]{:T(128)} %bitcast.31, f32[]{:T(128)} %bitcast.30, f32[]{:T(128)} %bitcast.29, f32[]{:T(128)} %bitcast.28, f32[]{:T(128)} %bitcast.27, f32[]{:T(128)} %bitcast.26, f32[]{:T(128)} %bitcast.25, f32[]{:T(128)} %bitcast.24, ...), kind=kLoop, calls=%fused_computation.1946 | loop fusion | flops 1900544 | bytes 524348 | tf_op jit(solution)/shard_map/add | solution.py:30
  113.2 10.4 %fusion.1142 = f32[16,32,128]{2,1,0:T(8,128)S(1)} fusion(f32[16,32,128]{2,1,0:T(8,128)S(1)} %fusion.687, f32[]{:T(128)} %bitcast.32, f32[]{:T(128)} %bitcast.31, f32[]{:T(128)} %bitcast.30, f32[]{:T(128)} %bitcast.29, f32[]{:T(128)} %bitcast.28, f32[]{:T(128)} %bitcast.27, f32[]{:T(128)} %bitcast.26, f32[]{:T(128)} %bitcast.25, f32[]{:T(128)} %bitcast.24, ...), kind=kLoop, calls=%fused_computation.1974 | loop fusion | flops 1900544 | bytes 524348 | tf_op jit(solution)/shard_map/add | solution.py:30
  134.7 10.8 %fusion.504 = f32[16,32,128]{2,1,0:T(8,128)S(1)} fusion(f32[16,32,128]{2,1,0:T(8,128)S(1)} %fusion.1142, f32[16,7,128]{2,1,0:T(8,128)S(1)} %collective-permute-done.6, f32[16,7,128]{2,1,0:T(8,128)S(1)} %collective-permute-done.5, f32[1,128,32,128]{3,2,1,0:T(8,128)} %param.4, s32[]{:T(128)S(6)} %select_n.62, f32[]{:T(128)} %bitcast.45, f32[]{:T(128)} %bitcast.44, ...), kind=kLoop, calls=%fused_computation.1336 | loop fusion | flops 2883584 | bytes 901184 | tf_op jit(solution)/shard_map/div | solution.py:55
  166.5 10.4 %fusion.1170 = f32[16,32,128]{2,1,0:T(8,128)S(1)} fusion(f32[16,32,128]{2,1,0:T(8,128)S(1)} %fusion.465, f32[]{:T(128)} %bitcast.32, f32[]{:T(128)} %bitcast.31, f32[]{:T(128)} %bitcast.30, f32[]{:T(128)} %bitcast.29, f32[]{:T(128)} %bitcast.28, f32[]{:T(128)} %bitcast.27, f32[]{:T(128)} %bitcast.26, f32[]{:T(128)} %bitcast.25, f32[]{:T(128)} %bitcast.24, ...), kind=kLoop, calls=%fused_computation.2002 | loop fusion | flops 1900544 | bytes 524348 | tf_op jit(solution)/shard_map/add | solution.py:30
  204.7 10.4 %fusion.1198 = f32[16,32,128]{2,1,0:T(8,128)S(1)} fusion(f32[16,32,128]{2,1,0:T(8,128)S(1)} %fusion.744, f32[]{:T(128)} %bitcast.32, f32[]{:T(128)} %bitcast.31, f32[]{:T(128)} %bitcast.30, f32[]{:T(128)} %bitcast.29, f32[]{:T(128)} %bitcast.28, f32[]{:T(128)} %bitcast.27, f32[]{:T(128)} %bitcast.26, f32[]{:T(128)} %bitcast.25, f32[]{:T(128)} %bitcast.24, ...), kind=kLoop, calls=%fused_computation.2030 | loop fusion | flops 1900544 | bytes 524348 | tf_op jit(solution)/shard_map/add | solution.py:30
  226.2 10.8 %fusion.427 = f32[16,32,128]{2,1,0:T(8,128)S(1)} fusion(f32[16,32,128]{2,1,0:T(8,128)S(1)} %fusion.1198, f32[16,7,128]{2,1,0:T(8,128)S(1)} %collective-permute-done.11, f32[16,7,128]{2,1,0:T(8,128)S(1)} %collective-permute-done.10, f32[1,128,32,128]{3,2,1,0:T(8,128)} %param.4, s32[]{:T(128)S(6)} %select_n.64, f32[]{:T(128)} %bitcast.45, f32[]{:T(128)} %bitcast.44, ...), kind=kLoop, calls=%fused_computation.1259 | loop fusion | flops 2883584 | bytes 901184 | tf_op jit(solution)/shard_map/div | solution.py:55
  297.8 10.4 %fusion.1254 = f32[16,32,128]{2,1,0:T(8,128)S(1)} fusion(f32[16,32,128]{2,1,0:T(8,128)S(1)} %fusion.801, f32[]{:T(128)} %bitcast.32, f32[]{:T(128)} %bitcast.31, f32[]{:T(128)} %bitcast.30, f32[]{:T(128)} %bitcast.29, f32[]{:T(128)} %bitcast.28, f32[]{:T(128)} %bitcast.27, f32[]{:T(128)} %bitcast.26, f32[]{:T(128)} %bitcast.25, f32[]{:T(128)} %bitcast.24, ...), kind=kLoop, calls=%fused_computation.2086 | loop fusion | flops 1900544 | bytes 524348 | tf_op jit(solution)/shard_map/add | solution.py:30
  319.3 10.8 %fusion.350 = f32[16,32,128]{2,1,0:T(8,128)S(1)} fusion(f32[16,32,128]{2,1,0:T(8,128)S(1)} %fusion.1254, f32[16,7,128]{2,1,0:T(8,128)S(1)} %collective-permute-done.16, f32[16,7,128]{2,1,0:T(8,128)S(1)} %collective-permute-done.15, f32[1,128,32,128]{3,2,1,0:T(8,128)} %param.4, s32[]{:T(128)S(6)} %select_n.66, f32[]{:T(128)} %bitcast.45, f32[]{:T(128)} %bitcast.44, ...), kind=kLoop, calls=%fused_computation.1182 | loop fusion | flops 2883584 | bytes 901184 | tf_op jit(solution)/shard_map/div | solution.py:55
  351.1 10.4 %fusion.1282 = f32[16,32,128]{2,1,0:T(8,128)S(1)} fusion(f32[16,32,128]{2,1,0:T(8,128)S(1)} %fusion.311, f32[]{:T(128)} %bitcast.32, f32[]{:T(128)} %bitcast.31, f32[]{:T(128)} %bitcast.30, f32[]{:T(128)} %bitcast.29, f32[]{:T(128)} %bitcast.28, f32[]{:T(128)} %bitcast.27, f32[]{:T(128)} %bitcast.26, f32[]{:T(128)} %bitcast.25, f32[]{:T(128)} %bitcast.24, ...), kind=kLoop, calls=%fused_computation.2114 | loop fusion | flops 1900544 | bytes 524348 | tf_op jit(solution)/shard_map/add | solution.py:30
  390.9 10.4 %fusion.1310 = f32[16,32,128]{2,1,0:T(8,128)S(1)} fusion(f32[16,32,128]{2,1,0:T(8,128)S(1)} %fusion.858, f32[]{:T(128)} %bitcast.32, f32[]{:T(128)} %bitcast.31, f32[]{:T(128)} %bitcast.30, f32[]{:T(128)} %bitcast.29, f32[]{:T(128)} %bitcast.28, f32[]{:T(128)} %bitcast.27, f32[]{:T(128)} %bitcast.26, f32[]{:T(128)} %bitcast.25, f32[]{:T(128)} %bitcast.24, ...), kind=kLoop, calls=%fused_computation.2142 | loop fusion | flops 1900544 | bytes 524348 | tf_op jit(solution)/shard_map/add | solution.py:30
  412.4 10.8 %fusion.273 = f32[16,32,128]{2,1,0:T(8,128)S(1)} fusion(f32[16,32,128]{2,1,0:T(8,128)S(1)} %fusion.1310, f32[16,7,128]{2,1,0:T(8,128)S(1)} %collective-permute-done.21, f32[16,7,128]{2,1,0:T(8,128)S(1)} %collective-permute-done.20, f32[1,128,32,128]{3,2,1,0:T(8,128)} %param.4, s32[]{:T(128)S(6)} %select_n.68, f32[]{:T(128)} %bitcast.45, f32[]{:T(128)} %bitcast.44, ...), kind=kLoop, calls=%fused_computation.1105 | loop fusion | flops 2883584 | bytes 901184 | tf_op jit(solution)/shard_map/div | solution.py:55
  444.2 10.4 %fusion.1338 = f32[16,32,128]{2,1,0:T(8,128)S(1)} fusion(f32[16,32,128]{2,1,0:T(8,128)S(1)} %fusion.234, f32[]{:T(128)} %bitcast.32, f32[]{:T(128)} %bitcast.31, f32[]{:T(128)} %bitcast.30, f32[]{:T(128)} %bitcast.29, f32[]{:T(128)} %bitcast.28, f32[]{:T(128)} %bitcast.27, f32[]{:T(128)} %bitcast.26, f32[]{:T(128)} %bitcast.25, f32[]{:T(128)} %bitcast.24, ...), kind=kLoop, calls=%fused_computation.2170 | loop fusion | flops 1900544 | bytes 524348 | tf_op jit(solution)/shard_map/add | solution.py:30
  484.0 10.4 %fusion.1366 = f32[16,32,128]{2,1,0:T(8,128)S(1)} fusion(f32[16,32,128]{2,1,0:T(8,128)S(1)} %fusion.915, f32[]{:T(128)} %bitcast.32, f32[]{:T(128)} %bitcast.31, f32[]{:T(128)} %bitcast.30, f32[]{:T(128)} %bitcast.29, f32[]{:T(128)} %bitcast.28, f32[]{:T(128)} %bitcast.27, f32[]{:T(128)} %bitcast.26, f32[]{:T(128)} %bitcast.25, f32[]{:T(128)} %bitcast.24, ...), kind=kLoop, calls=%fused_computation.2198 | loop fusion | flops 1900544 | bytes 524348 | tf_op jit(solution)/shard_map/add | solution.py:30
  505.5 10.8 %fusion.196 = f32[16,32,128]{2,1,0:T(8,128)S(1)} fusion(f32[16,32,128]{2,1,0:T(8,128)S(1)} %fusion.1366, f32[16,7,128]{2,1,0:T(8,128)S(1)} %collective-permute-done.26, f32[16,7,128]{2,1,0:T(8,128)S(1)} %collective-permute-done.25, f32[1,128,32,128]{3,2,1,0:T(8,128)} %param.4, s32[]{:T(128)S(6)} %select_n.70, f32[]{:T(128)} %bitcast.45, f32[]{:T(128)} %bitcast.44, ...), kind=kLoop, calls=%fused_computation.1028 | loop fusion | flops 2883584 | bytes 901184 | tf_op jit(solution)/shard_map/div | solution.py:55
  537.3 10.4 %fusion.1394 = f32[16,32,128]{2,1,0:T(8,128)S(1)} fusion(f32[16,32,128]{2,1,0:T(8,128)S(1)} %fusion.157, f32[]{:T(128)} %bitcast.32, f32[]{:T(128)} %bitcast.31, f32[]{:T(128)} %bitcast.30, f32[]{:T(128)} %bitcast.29, f32[]{:T(128)} %bitcast.28, f32[]{:T(128)} %bitcast.27, f32[]{:T(128)} %bitcast.26, f32[]{:T(128)} %bitcast.25, f32[]{:T(128)} %bitcast.24, ...), kind=kLoop, calls=%fused_computation.2226 | loop fusion | flops 1900544 | bytes 524348 | tf_op jit(solution)/shard_map/add | solution.py:30
  577.2 10.4 %fusion.1422 = f32[16,32,128]{2,1,0:T(8,128)S(1)} fusion(f32[16,32,128]{2,1,0:T(8,128)S(1)} %fusion.972, f32[]{:T(128)} %bitcast.32, f32[]{:T(128)} %bitcast.31, f32[]{:T(128)} %bitcast.30, f32[]{:T(128)} %bitcast.29, f32[]{:T(128)} %bitcast.28, f32[]{:T(128)} %bitcast.27, f32[]{:T(128)} %bitcast.26, f32[]{:T(128)} %bitcast.25, f32[]{:T(128)} %bitcast.24, ...), kind=kLoop, calls=%fused_computation.2254 | loop fusion | flops 1900544 | bytes 524348 | tf_op jit(solution)/shard_map/add | solution.py:30
  598.7 10.8 %fusion.119 = f32[16,32,128]{2,1,0:T(8,128)S(1)} fusion(f32[16,32,128]{2,1,0:T(8,128)S(1)} %fusion.1422, f32[16,7,128]{2,1,0:T(8,128)S(1)} %collective-permute-done.31, f32[16,7,128]{2,1,0:T(8,128)S(1)} %collective-permute-done.30, f32[1,128,32,128]{3,2,1,0:T(8,128)} %param.4, s32[]{:T(128)S(6)} %select_n.72, f32[]{:T(128)} %bitcast.45, f32[]{:T(128)} %bitcast.44, ...), kind=kLoop, calls=%fused_computation.951 | loop fusion | flops 2883584 | bytes 901184 | tf_op jit(solution)/shard_map/div | solution.py:55
  630.4 10.4 %fusion.1450 = f32[16,32,128]{2,1,0:T(8,128)S(1)} fusion(f32[16,32,128]{2,1,0:T(8,128)S(1)} %fusion.80, f32[]{:T(128)} %bitcast.32, f32[]{:T(128)} %bitcast.31, f32[]{:T(128)} %bitcast.30, f32[]{:T(128)} %bitcast.29, f32[]{:T(128)} %bitcast.28, f32[]{:T(128)} %bitcast.27, f32[]{:T(128)} %bitcast.26, f32[]{:T(128)} %bitcast.25, f32[]{:T(128)} %bitcast.24, ...), kind=kLoop, calls=%fused_computation.2282 | loop fusion | flops 1900544 | bytes 524348 | tf_op jit(solution)/shard_map/add | solution.py:30
  670.3 10.4 %fusion.1478 = f32[16,32,128]{2,1,0:T(8,128)S(1)} fusion(f32[16,32,128]{2,1,0:T(8,128)S(1)} %fusion.1029, f32[]{:T(128)} %bitcast.32, f32[]{:T(128)} %bitcast.31, f32[]{:T(128)} %bitcast.30, f32[]{:T(128)} %bitcast.29, f32[]{:T(128)} %bitcast.28, f32[]{:T(128)} %bitcast.27, f32[]{:T(128)} %bitcast.26, f32[]{:T(128)} %bitcast.25, f32[]{:T(128)} %bitcast.24, ...), kind=kLoop, calls=%fused_computation.2310 | loop fusion | flops 1900544 | bytes 524348 | tf_op jit(solution)/shard_map/add | solution.py:30
  691.8 10.8 %fusion.42 = f32[16,32,128]{2,1,0:T(8,128)S(1)} fusion(f32[16,32,128]{2,1,0:T(8,128)S(1)} %fusion.1478, f32[16,7,128]{2,1,0:T(8,128)S(1)} %collective-permute-done.36, f32[16,7,128]{2,1,0:T(8,128)S(1)} %collective-permute-done.35, f32[1,128,32,128]{3,2,1,0:T(8,128)} %param.4, s32[]{:T(128)S(6)} %select_n.74, f32[]{:T(128)} %bitcast.45, f32[]{:T(128)} %bitcast.44, ...), kind=kLoop, calls=%fused_computation.874 | loop fusion | flops 2883584 | bytes 901184 | tf_op jit(solution)/shard_map/div | solution.py:55
  (126 shorter events, 497.4 us)
Async XLA Ops:
  28.2 13.6 %collective-permute-start = (f32[16,7,128]{2,1,0:T(8,128)S(1)}, f32[16,7,128]{2,1,0:T(8,128)S(1)}, u32[]{:S(2)}, u32[]{:S(2)}) collective-permute-start(f32[16,7,128]{2,1,0:T(8,128)S(1)} %get-tuple-element.35), channel_id=1, source_target_pairs={{0,1},{1,2},{2,3},{3,4},{4,5},{5,6},{6,7},{7,8},{8,9},{9,10},{10,1... | collective-permute-start | bytes 172040 | tf_op jit(solution)/shard_map/ppermute | solution.py:14
  30.2 13.6 %collective-permute-start.1 = (f32[16,7,128]{2,1,0:T(8,128)S(1)}, f32[16,7,128]{2,1,0:T(8,128)S(1)}, u32[]{:S(2)}, u32[]{:S(2)}) collective-permute-start(f32[16,7,128]{2,1,0:T(8,128)S(1)} %get-tuple-element.36), channel_id=1, source_target_pairs={{1,0},{2,1},{3,2},{4,3},{5,4},{6,5},{7,6},{8,7},{9,8},{10,9},{11,1... | collective-permute-start | bytes 172040 | tf_op jit(solution)/shard_map/ppermute | solution.py:15
  54.5 9.2 %collective-permute-start.2 = (f32[16,7,128]{2,1,0:T(8,128)S(1)}, f32[16,7,128]{2,1,0:T(8,128)S(1)}, u32[]{:S(2)}, u32[]{:S(2)}) collective-permute-start(f32[16,7,128]{2,1,0:T(8,128)S(1)} %get-tuple-element.33), channel_id=1, source_target_pairs={{0,1},{1,2},{2,3},{3,4},{4,5},{5,6},{6,7},{7,8},{8,9},{9,10},{10,1... | collective-permute-start | bytes 172040 | tf_op jit(solution)/shard_map/ppermute | solution.py:14
  123.7 9.2 %collective-permute-start.5 = (f32[16,7,128]{2,1,0:T(8,128)S(1)}, f32[16,7,128]{2,1,0:T(8,128)S(1)}, u32[]{:S(2)}, u32[]{:S(2)}) collective-permute-start(f32[16,7,128]{2,1,0:T(8,128)S(1)} %get-tuple-element.31), channel_id=1, source_target_pairs={{0,1},{1,2},{2,3},{3,4},{4,5},{5,6},{6,7},{7,8},{8,9},{9,10},{10,1... | collective-permute-start | bytes 172040 | tf_op jit(solution)/shard_map/ppermute | solution.py:14
  145.6 9.2 %collective-permute-start.7 = (f32[16,7,128]{2,1,0:T(8,128)S(1)}, f32[16,7,128]{2,1,0:T(8,128)S(1)}, u32[]{:S(2)}, u32[]{:S(2)}) collective-permute-start(f32[16,7,128]{2,1,0:T(8,128)S(1)} %get-tuple-element.29), channel_id=1, source_target_pairs={{0,1},{1,2},{2,3},{3,4},{4,5},{5,6},{6,7},{7,8},{8,9},{9,10},{10,1... | collective-permute-start | bytes 172040 | tf_op jit(solution)/shard_map/ppermute | solution.py:14
  215.1 9.2 %collective-permute-start.10 = (f32[16,7,128]{2,1,0:T(8,128)S(1)}, f32[16,7,128]{2,1,0:T(8,128)S(1)}, u32[]{:S(2)}, u32[]{:S(2)}) collective-permute-start(f32[16,7,128]{2,1,0:T(8,128)S(1)} %get-tuple-element.27), channel_id=1, source_target_pairs={{0,1},{1,2},{2,3},{3,4},{4,5},{5,6},{6,7},{7,8},{8,9},{9,10},{10,1... | collective-permute-start | bytes 172040 | tf_op jit(solution)/shard_map/ppermute | solution.py:14
  237.0 9.4 %collective-permute-start.12 = (f32[16,7,128]{2,1,0:T(8,128)S(1)}, f32[16,7,128]{2,1,0:T(8,128)S(1)}, u32[]{:S(2)}, u32[]{:S(2)}) collective-permute-start(f32[16,7,128]{2,1,0:T(8,128)S(1)} %get-tuple-element.25), channel_id=1, source_target_pairs={{0,1},{1,2},{2,3},{3,4},{4,5},{5,6},{6,7},{7,8},{8,9},{9,10},{10,1... | collective-permute-start | bytes 172040 | tf_op jit(solution)/shard_map/ppermute | solution.py:14
  277.9 10.4 %collective-permute-start.14 = (f32[16,32,128]{2,1,0:T(8,128)S(1)}, f32[16,32,128]{2,1,0:T(8,128)S(1)}, u32[]{:S(2)}, u32[]{:S(2)}) collective-permute-start(f32[16,32,128]{2,1,0:T(8,128)S(1)} %fusion.773), channel_id=1, source_target_pairs={{0,64},{64,128},{128,192},{192,256},{256,320},{320,384},{384,448},... | collective-permute-start | bytes 786440 | tf_op jit(solution)/shard_map/ppermute | solution.py:22
  308.2 9.2 %collective-permute-start.15 = (f32[16,7,128]{2,1,0:T(8,128)S(1)}, f32[16,7,128]{2,1,0:T(8,128)S(1)}, u32[]{:S(2)}, u32[]{:S(2)}) collective-permute-start(f32[16,7,128]{2,1,0:T(8,128)S(1)} %get-tuple-element.23), channel_id=1, source_target_pairs={{0,1},{1,2},{2,3},{3,4},{4,5},{5,6},{6,7},{7,8},{8,9},{9,10},{10,1... | collective-permute-start | bytes 172040 | tf_op jit(solution)/shard_map/ppermute | solution.py:14
  330.1 9.2 %collective-permute-start.17 = (f32[16,7,128]{2,1,0:T(8,128)S(1)}, f32[16,7,128]{2,1,0:T(8,128)S(1)}, u32[]{:S(2)}, u32[]{:S(2)}) collective-permute-start(f32[16,7,128]{2,1,0:T(8,128)S(1)} %get-tuple-element.21), channel_id=1, source_target_pairs={{0,1},{1,2},{2,3},{3,4},{4,5},{5,6},{6,7},{7,8},{8,9},{9,10},{10,1... | collective-permute-start | bytes 172040 | tf_op jit(solution)/shard_map/ppermute | solution.py:14
  371.0 10.4 %collective-permute-start.19 = (f32[16,32,128]{2,1,0:T(8,128)S(1)}, f32[16,32,128]{2,1,0:T(8,128)S(1)}, u32[]{:S(2)}, u32[]{:S(2)}) collective-permute-start(f32[16,32,128]{2,1,0:T(8,128)S(1)} %fusion.830), channel_id=1, source_target_pairs={{0,64},{64,128},{128,192},{192,256},{256,320},{320,384},{384,448},... | collective-permute-start | bytes 786440 | tf_op jit(solution)/shard_map/ppermute | solution.py:22
  401.3 9.2 %collective-permute-start.20 = (f32[16,7,128]{2,1,0:T(8,128)S(1)}, f32[16,7,128]{2,1,0:T(8,128)S(1)}, u32[]{:S(2)}, u32[]{:S(2)}) collective-permute-start(f32[16,7,128]{2,1,0:T(8,128)S(1)} %get-tuple-element.19), channel_id=1, source_target_pairs={{0,1},{1,2},{2,3},{3,4},{4,5},{5,6},{6,7},{7,8},{8,9},{9,10},{10,1... | collective-permute-start | bytes 172040 | tf_op jit(solution)/shard_map/ppermute | solution.py:14
  423.2 9.2 %collective-permute-start.22 = (f32[16,7,128]{2,1,0:T(8,128)S(1)}, f32[16,7,128]{2,1,0:T(8,128)S(1)}, u32[]{:S(2)}, u32[]{:S(2)}) collective-permute-start(f32[16,7,128]{2,1,0:T(8,128)S(1)} %get-tuple-element.17), channel_id=1, source_target_pairs={{0,1},{1,2},{2,3},{3,4},{4,5},{5,6},{6,7},{7,8},{8,9},{9,10},{10,1... | collective-permute-start | bytes 172040 | tf_op jit(solution)/shard_map/ppermute | solution.py:14
  464.1 10.4 %collective-permute-start.24 = (f32[16,32,128]{2,1,0:T(8,128)S(1)}, f32[16,32,128]{2,1,0:T(8,128)S(1)}, u32[]{:S(2)}, u32[]{:S(2)}) collective-permute-start(f32[16,32,128]{2,1,0:T(8,128)S(1)} %fusion.887), channel_id=1, source_target_pairs={{0,64},{64,128},{128,192},{192,256},{256,320},{320,384},{384,448},... | collective-permute-start | bytes 786440 | tf_op jit(solution)/shard_map/ppermute | solution.py:22
  494.5 9.4 %collective-permute-start.25 = (f32[16,7,128]{2,1,0:T(8,128)S(1)}, f32[16,7,128]{2,1,0:T(8,128)S(1)}, u32[]{:S(2)}, u32[]{:S(2)}) collective-permute-start(f32[16,7,128]{2,1,0:T(8,128)S(1)} %get-tuple-element.15), channel_id=1, source_target_pairs={{0,1},{1,2},{2,3},{3,4},{4,5},{5,6},{6,7},{7,8},{8,9},{9,10},{10,1... | collective-permute-start | bytes 172040 | tf_op jit(solution)/shard_map/ppermute | solution.py:14
  516.3 9.2 %collective-permute-start.27 = (f32[16,7,128]{2,1,0:T(8,128)S(1)}, f32[16,7,128]{2,1,0:T(8,128)S(1)}, u32[]{:S(2)}, u32[]{:S(2)}) collective-permute-start(f32[16,7,128]{2,1,0:T(8,128)S(1)} %get-tuple-element.13), channel_id=1, source_target_pairs={{0,1},{1,2},{2,3},{3,4},{4,5},{5,6},{6,7},{7,8},{8,9},{9,10},{10,1... | collective-permute-start | bytes 172040 | tf_op jit(solution)/shard_map/ppermute | solution.py:14
  518.3 9.2 %collective-permute-start.28 = (f32[16,7,128]{2,1,0:T(8,128)S(1)}, f32[16,7,128]{2,1,0:T(8,128)S(1)}, u32[]{:S(2)}, u32[]{:S(2)}) collective-permute-start(f32[16,7,128]{2,1,0:T(8,128)S(1)} %get-tuple-element.14), channel_id=1, source_target_pairs={{1,0},{2,1},{3,2},{4,3},{5,4},{6,5},{7,6},{8,7},{9,8},{10,9},{11,1... | collective-permute-start | bytes 172040 | tf_op jit(solution)/shard_map/ppermute | solution.py:15
  557.2 10.4 %collective-permute-start.29 = (f32[16,32,128]{2,1,0:T(8,128)S(1)}, f32[16,32,128]{2,1,0:T(8,128)S(1)}, u32[]{:S(2)}, u32[]{:S(2)}) collective-permute-start(f32[16,32,128]{2,1,0:T(8,128)S(1)} %fusion.944), channel_id=1, source_target_pairs={{0,64},{64,128},{128,192},{192,256},{256,320},{320,384},{384,448},... | collective-permute-start | bytes 786440 | tf_op jit(solution)/shard_map/ppermute | solution.py:22
  587.6 9.2 %collective-permute-start.30 = (f32[16,7,128]{2,1,0:T(8,128)S(1)}, f32[16,7,128]{2,1,0:T(8,128)S(1)}, u32[]{:S(2)}, u32[]{:S(2)}) collective-permute-start(f32[16,7,128]{2,1,0:T(8,128)S(1)} %get-tuple-element.11), channel_id=1, source_target_pairs={{0,1},{1,2},{2,3},{3,4},{4,5},{5,6},{6,7},{7,8},{8,9},{9,10},{10,1... | collective-permute-start | bytes 172040 | tf_op jit(solution)/shard_map/ppermute | solution.py:14
  609.5 9.4 %collective-permute-start.32 = (f32[16,7,128]{2,1,0:T(8,128)S(1)}, f32[16,7,128]{2,1,0:T(8,128)S(1)}, u32[]{:S(2)}, u32[]{:S(2)}) collective-permute-start(f32[16,7,128]{2,1,0:T(8,128)S(1)} %get-tuple-element.9), channel_id=1, source_target_pairs={{0,1},{1,2},{2,3},{3,4},{4,5},{5,6},{6,7},{7,8},{8,9},{9,10},{10,1... | collective-permute-start | bytes 172040 | tf_op jit(solution)/shard_map/ppermute | solution.py:14
  650.4 10.4 %collective-permute-start.34 = (f32[16,32,128]{2,1,0:T(8,128)S(1)}, f32[16,32,128]{2,1,0:T(8,128)S(1)}, u32[]{:S(2)}, u32[]{:S(2)}) collective-permute-start(f32[16,32,128]{2,1,0:T(8,128)S(1)} %fusion.1001), channel_id=1, source_target_pairs={{0,64},{64,128},{128,192},{192,256},{256,320},{320,384},{384,448},... | collective-permute-start | bytes 786440 | tf_op jit(solution)/shard_map/ppermute | solution.py:22
  680.7 9.2 %collective-permute-start.35 = (f32[16,7,128]{2,1,0:T(8,128)S(1)}, f32[16,7,128]{2,1,0:T(8,128)S(1)}, u32[]{:S(2)}, u32[]{:S(2)}) collective-permute-start(f32[16,7,128]{2,1,0:T(8,128)S(1)} %get-tuple-element.7), channel_id=1, source_target_pairs={{0,1},{1,2},{2,3},{3,4},{4,5},{5,6},{6,7},{7,8},{8,9},{9,10},{10,1... | collective-permute-start | bytes 172040 | tf_op jit(solution)/shard_map/ppermute | solution.py:14
  702.6 9.2 %collective-permute-start.37 = (f32[16,7,128]{2,1,0:T(8,128)S(1)}, f32[16,7,128]{2,1,0:T(8,128)S(1)}, u32[]{:S(2)}, u32[]{:S(2)}) collective-permute-start(f32[16,7,128]{2,1,0:T(8,128)S(1)} %get-tuple-element.5), channel_id=1, source_target_pairs={{0,1},{1,2},{2,3},{3,4},{4,5},{5,6},{6,7},{7,8},{8,9},{9,10},{10,1... | collective-permute-start | bytes 172040 | tf_op jit(solution)/shard_map/ppermute | solution.py:14
  743.5 10.4 %collective-permute-start.39 = (f32[16,32,128]{2,1,0:T(8,128)S(1)}, f32[16,32,128]{2,1,0:T(8,128)S(1)}, u32[]{:S(2)}, u32[]{:S(2)}) collective-permute-start(f32[16,32,128]{2,1,0:T(8,128)S(1)} %fusion.1058), channel_id=1, source_target_pairs={{0,64},{64,128},{128,192},{192,256},{256,320},{320,384},{384,448},... | collective-permute-start | bytes 786440 | tf_op jit(solution)/shard_map/ppermute | solution.py:22
  (17 other events, 231.3 us)
where the time goes:
time: 766 us; the launch traced here: 755 us
  other arithmetic  487 us (64%)
  starting transfers between devices  174 us (23%)
  waiting for transfers between devices  87.2 us (11%)
    add x32, other arithmetic, valid_pass(): summed + kernel[offset] * lax.slice_in_dim(padded, offset, offset + exten...  324 us
    ppermute x16, starting transfers between devices, extended(): after = lax.ppermute(first, axis, down)  121 us
    div x8, other arithmetic, update_rims(): quotient = observed / blurred  86.3 us
    mul x8, other arithmetic, update_rims(): return current * backward  76.4 us
    ppermute x8, waiting for transfers between devices, from_behind(): lax.ppermute(value, axis, [(i, (i + by) % size) for i in range(size)])  57.7 us
    ppermute x16, starting transfers between devices, extended(): before = lax.ppermute(last, axis, up)  30.7 us
    ppermute x16, waiting for transfers between devices, extended(): after = lax.ppermute(first, axis, down)  29.3 us
    ppermute x8, starting transfers between devices, from_behind(): lax.ppermute(value, axis, [(i, (i + by) % size) for i in range(size)])  21.5 us
  transfers between devices with their start and end apart: 40, of which 25 were waited for; matrix products, arithmetic and copies ran while one was open for 0% of the time, Pallas kernels for 0%

commit v1 on v0

v1 whole, which is shorter than its diff:
```python
import functools

import jax
import jax.numpy as jnp
from jax import lax
from jax.experimental import pallas as pl
from jax.experimental.pallas import tpu as pltpu
from jax.sharding import PartitionSpec as P

MESH = pl.DeviceIdType.MESH
TAPS = 15
RADIUS = 7
STEP = 8
WIDE = 3 * STEP
AHEAD = 3


def split(value):
    high = value.astype(jnp.bfloat16)
    low = (value - high.astype(jnp.float32)).astype(jnp.bfloat16)
    return high, low


def dot(a, b):
    return jnp.dot(a, b, preferred_element_type=jnp.float32)


def offsets(depth, width):
    lanes = depth * WIDE
    column = lax.broadcasted_iota(jnp.int32, (depth, lanes), 1)
    plane = (column * 2731) >> 16
    dz = plane - lax.broadcasted_iota(jnp.int32, (depth, lanes), 0)
    column = lax.broadcasted_iota(jnp.int32, (STEP, lanes), 1)
    row = column - ((column * 2731) >> 16) * WIDE
    dx = row - lax.broadcasted_iota(jnp.int32, (STEP, lanes), 0) - STEP
    dy = lax.broadcasted_iota(jnp.int32, (width, width), 0) - lax.broadcasted_iota(
        jnp.int32, (width, width), 1
    )
    return dz, dx, dy


def banded(difference, taps, sign):
    result = jnp.zeros(difference.shape, jnp.float32)
    for k in range(TAPS):
        result = jnp.where(difference == sign * (k - RADIUS), taps[:, k : k + 1], result)
    return result


def matrices(profile, dz, dx, dy, sign):
    gz = banded(dz, profile[0:1], sign)
    gx = banded(dx, profile[1:2], sign)
    left = (gz[:, None, :] * gx[None, :, :]).reshape(dz.shape[0] * STEP, dz.shape[1])
    return split(left), split(banded(dy, profile[2:3], sign))


def correlate(block, left, left_high, right_high, right_low):
    depth, _, width = block.shape
    rows = depth * STEP
    flat = [block[:, i * STEP : i * STEP + WIDE, :].reshape(depth * WIDE, width) for i in (0, 1)]
    high, low = split(jnp.concatenate(flat, axis=1))
    both = dot(left, high)
    mid = both[:rows] + (both[rows:] + dot(left_high, low))
    mid = jnp.concatenate([mid[:, :width], mid[:, width:]], axis=0)
    high, low = split(mid)
    out = dot(high, right_high) + (dot(low, right_high) + dot(high, right_low))
    return [out[i * rows : (i + 1) * rows].reshape(depth, STEP, width) for i in (0, 1)]


def kernel(views, tiles, est, img, prof, out, ext, shots, quot, prof_all, zx, yy,
           load_sem, s_send, s_recv, i_send, i_recv, p_send, p_recv):
    view, tile = lax.axis_index("view"), lax.axis_index("tile")
    depth, rows, width = est.shape
    half = rows // 2
    wide = depth * STEP

    def around(value, size):
        return lax.rem(value + size, size)

    barrier = pltpu.get_barrier_semaphore()
    for dv in range(views):
        for dt in (0, 1, -1):
            if dv or dt:
                pl.semaphore_signal(
                    barrier, inc=1, device_id=(around(view + dv, views), around(tile + dt, tiles)),
                    device_id_type=MESH,
                )

    def own_image():
        return pltpu.make_async_copy(
            img.at[pl.ds(pl.multiple_of(view * depth, depth), depth)],
            shots.at[0, :, pl.ds(STEP, rows), :], load_sem.at[0])

    def own_slab():
        return pltpu.make_async_copy(est, ext.at[0, :, pl.ds(half, rows), :], load_sem.at[1])

    own_image().start()
    own_slab().start()

    def rim(n, side, first=False):
        here = pl.multiple_of(half * side, half)
        source = est.at[:, pl.ds(here, half), :] if first else ext.at[
            n, :, pl.ds(pl.multiple_of(half + half * side, half), half), :]
        return pltpu.make_async_remote_copy(
            src_ref=source,
            dst_ref=ext.at[n, :, pl.ds(pl.multiple_of((half + rows) * (1 - side), half), half), :],
            send_sem=s_send.at[n, side], recv_sem=s_recv.at[n, side],
            device_id=(view, around(tile + 2 * side - 1, tiles)), device_id_type=MESH)

    def block(n):
        to = around(view - n, views)
        return to, pl.ds(pl.multiple_of(to * depth, depth), depth)

    def shot(n):
        to, planes = block(n)
        return pltpu.make_async_remote_copy(
            src_ref=img.at[planes], dst_ref=shots.at[n, :, pl.ds(STEP, rows), :],
            send_sem=i_send.at[n, 2], recv_sem=i_recv.at[n, 2],
            device_id=(to, tile), device_id_type=MESH)

    def shot_rim(n, side):
        to, planes = block(n)
        here = pl.multiple_of((rows - STEP) * side, STEP)
        there = pl.multiple_of((rows + STEP) * (1 - side), STEP)
        return pltpu.make_async_remote_copy(
            src_ref=img.at[planes, pl.ds(here, STEP), :],
            dst_ref=shots.at[n, :, pl.ds(there, STEP), :],
            send_sem=i_send.at[n, side], recv_sem=i_recv.at[n, side],
            device_id=(to, around(tile + 2 * side - 1, tiles)), device_id_type=MESH)

    def taps(n):
        return pltpu.make_async_remote_copy(
            src_ref=prof, dst_ref=prof_all.at[n], send_sem=p_send.at[n], recv_sem=p_recv.at[n],
            device_id=(around(view - n, views), tile), device_id_type=MESH)

    def send_shots(n):
        shot(n).start()
        shot_rim(n, 0).start()
        shot_rim(n, 1).start()

    prof_all[0] = prof[...]
    dz, dx, dy = offsets(depth, width)
    pl.semaphore_wait(barrier, 3 * views - 1)

    for side in (0, 1):
        rim(0, side, True).start()
    for side in (0, 1):
        shot_rim(0, side).start()
    for n in range(1, views):
        taps(n).start()
    for n in range(1, AHEAD):
        send_shots(n)
    own_image().wait()
    own_slab().wait()

    def forward(n, start):
        got = correlate(ext[n, :, pl.ds(start, rows), :], zx[0], zx[0, :wide], yy[0, 0], yy[0, 1])
        return [shots[n, :, pl.ds(start + i * STEP, STEP), :] / got[i] for i in (0, 1)]

    odd = lax.rem(tile, 2)

    def update(n, carry):
        @pl.when(n + AHEAD < views)
        def _():
            send_shots(n + AHEAD)

        @pl.when(n > 0)
        def _():
            taps(n).wait_recv()

        profile = prof_all[n]
        for which, sign in ((0, 1), (1, -1)):
            left, right = matrices(profile, dz, dx, dy, sign)
            zx[which, :wide] = left[0]
            zx[which, wide:] = left[1]
            yy[which, 0] = right[0]
            yy[which, 1] = right[1]

        @pl.when(n > 0)
        def _():
            shot(n).wait_recv()

        inner = forward(n, half)
        for i in (0, 1):
            quot[:, half + i * STEP : half + (i + 1) * STEP, :] = inner[i]

        def one_side(number, carry):
            side = number * odd + (1 - number) * (1 - odd)
            edge = tile == side * (tiles - 1)
            start = pl.multiple_of(side * rows, rows)
            rim(n, 1 - side).wait_recv()
            shot_rim(n, 1 - side).wait_recv()

            @pl.when(edge)
            def _():
                ext[n, :, pl.ds(pl.multiple_of((half + rows) * side, half), half), :] = jnp.zeros(
                    (depth, half, width), jnp.float32)

            got = forward(n, start)
            for i in (0, 1):
                value = jnp.where(jnp.logical_and(edge, side == i), 0.0, got[i])
                quot[:, pl.ds(pl.multiple_of(start + i * STEP, STEP), STEP), :] = value
            begin = pl.multiple_of(side * half, half)
            got = correlate(quot[:, pl.ds(begin, rows), :], zx[1], zx[1, :wide], yy[1, 0], yy[1, 1])
            for i in (0, 1):
                place = pl.ds(pl.multiple_of(half + begin + i * STEP, STEP), STEP)
                ext[n + 1, :, place, :] = ext[n, :, place, :] * got[i]

            @pl.when(n < views - 1)
            def _():
                rim(n + 1, side).start()

            return carry

        return lax.fori_loop(0, 2, one_side, carry)

    lax.fori_loop(0, views, update, 0)
    out[...] = ext[views, :, pl.ds(half, rows), :]

    def drain(n, carry):
        for side in (0, 1):
            rim(n, side).wait_send()
            shot_rim(n, side).wait_send()

        @pl.when(n > 0)
        def _():
            shot(n).wait_send()
            taps(n).wait_send()

        return carry

    lax.fori_loop(0, views, drain, 0)


def shards(views, tiles, estimate, images, profiles):
    depth, rows, width = estimate.shape
    profile = jnp.pad(profiles[0], ((0, 5), (0, width - TAPS)))
    anywhere, vmem = (pl.BlockSpec(memory_space=space) for space in (pl.ANY, pltpu.VMEM))
    return pl.pallas_call(
        functools.partial(kernel, views, tiles),
        out_shape=jax.ShapeDtypeStruct(estimate.shape, estimate.dtype),
        in_specs=[anywhere, anywhere, vmem],
        out_specs=vmem,
        scratch_shapes=[
            pltpu.VMEM((views + 1, depth, 2 * rows, width), jnp.float32),
            pltpu.VMEM((views, depth, rows + 2 * STEP, width), jnp.float32),
            pltpu.VMEM((depth, rows + 2 * STEP, width), jnp.float32),
            pltpu.VMEM((views, 8, width), jnp.float32),
            pltpu.VMEM((2, 2 * depth * STEP, depth * WIDE), jnp.bfloat16),
            pltpu.VMEM((2, 2, width, width), jnp.bfloat16),
            pltpu.SemaphoreType.DMA((2,)),
            pltpu.SemaphoreType.DMA((views, 2)),
            pltpu.SemaphoreType.DMA((views, 2)),
            pltpu.SemaphoreType.DMA((views, 3)),
            pltpu.SemaphoreType.DMA((views, 3)),
            pltpu.SemaphoreType.DMA((views,)),
            pltpu.SemaphoreType.DMA((views,)),
        ],
        compiler_params=pltpu.CompilerParams(
            collective_id=0, has_side_effects=True, vmem_limit_bytes=48 << 20),
    )(estimate, images[0], profile)


def solution(mesh):
    return jax.shard_map(
        functools.partial(shards, mesh.shape["view"], mesh.shape["tile"]),
        mesh=mesh,
        in_specs=(P("view", "tile", None), P("view", None, "tile", None), P("view", None, None)),
        out_specs=P("view", "tile", None),
        check_vma=False,
    )
```

time: 766 us -> 81.3 us (0.11); the launches traced: 755 us -> 81.1 us
  other arithmetic: 487 us -> 0 us
  starting transfers between devices: 174 us -> 0 us
  waiting for transfers between devices: 87.2 us -> 0 us
  Pallas kernels: 0 us -> 77.2 us
    add x32 -> x0, other arithmetic: 324 us -> none  [valid_pass(): summed + kernel[offset] * lax.slice_in_dim(padded, offset, offset + exten...]
    ppermute x40 -> x0, starting transfers between devices: 174 us -> none  [the longest x16 121 us: extended(): after = lax.ppermute(first, axis, down)]
    ppermute x40 -> x0, waiting for transfers between devices: 87.2 us -> none  [the longest x8 57.7 us: from_behind(): lax.ppermute(value, axis, [(i, (i + by) % size) for i in range(size)])]
    div x8 -> x0, other arithmetic: 86.3 us -> none  [update_rims(): quotient = observed / blurred]
    pallas_call x0 -> x1, Pallas kernels: none -> 77.2 us  [shards(): pl.pallas_call(functools.partial(kernel, views, tiles), out_shape=jax.Sha...]
    mul x8 -> x0, other arithmetic: 76.4 us -> none  [update_rims(): return current * backward]
  transfers between devices with their start and end apart: 40 -> 0, of which waited for: 25 -> 0; matrix products, arithmetic and copies ran while one was open for 0% -> 0% of each run, Pallas kernels for 0% -> 0%
where the time goes in v1:
time: 81.3 us; the launch traced here: 81.1 us
  Pallas kernels  77.2 us (95%)
  local copies, waits for them, and re-layouts  3.93 us (5%)
    pallas_call x1, Pallas kernels, shards(): pl.pallas_call(functools.partial(kernel, views, tiles), out_shape=jax.Sha...  77.2 us
    unnamed x6, local copies, waits for them, and re-layouts  3.93 us

profile of v1, /device:TPU:6, one launch (start us, length us, event | category | flops | bytes accessed | tf_op | source)
XLA Modules:
  0.0 81.1 jit_solution(17179371960471365778)
XLA Ops:
  0.0 0.7 copy.6
  0.7 0.0 copy-start
  0.7 1.6 %copy-done = f32[1,128,32,128]{3,2,1,0:T(8,128)S(1)} copy-done((f32[1,128,32,128]{3,2,1,0:T(8,128)S(1)}, f32[1,128,32,128]{3,2,1,0:T(8,128)}, u32[]{:S(2)}) %copy-start) | copy-done | bytes 2097176
  2.3 0.0 copy-start.1
  2.3 0.9 %copy-done.1 = f32[16,32,128]{2,1,0:T(8,128)S(1)} copy-done((f32[16,32,128]{2,1,0:T(8,128)S(1)}, f32[16,32,128]{2,1,0:T(8,128)}, u32[]{:S(2)}) %copy-start.1) | copy-done | bytes 262168
  3.2 77.2 %shard_map.37 = f32[16,32,128]{2,1,0:T(8,128)S(1)} custom-call(f32[16,32,128]{2,1,0:T(8,128)S(1)} %copy-done.1, f32[128,32,128]{2,1,0:T(8,128)S(1)} %bitcast.4, f32[8,128]{1,0:T(8,128)S(1)} %pad.4.prof), custom_call_target="tpu_custom_call" | custom-call | tf_op jit(solution)/shard_map/pallas_call | solution.py:238
  80.4 0.7 copy.8
  (1 shorter events, 0.0 us)
Async XLA Ops:
  0.7 1.6 %copy-start = (f32[1,128,32,128]{3,2,1,0:T(8,128)S(1)}, f32[1,128,32,128]{3,2,1,0:T(8,128)}, u32[]{:S(2)}) copy-start(f32[1,128,32,128]{3,2,1,0:T(8,128)} %param.4) | copy-start | bytes 6291460
  2.3 0.9 %copy-start.1 = (f32[16,32,128]{2,1,0:T(8,128)S(1)}, f32[16,32,128]{2,1,0:T(8,128)}, u32[]{:S(2)}) copy-start(f32[16,32,128]{2,1,0:T(8,128)} %est.1) | copy-start | bytes 786436

commit v2 on v1

--- a/solution.py
+++ b/solution.py
@@ -47,10 +47,10 @@
 
 
 def matrices(profile, dz, dx, dy, sign):
-    gz = banded(dz, profile[0:1], sign)
-    gx = banded(dx, profile[1:2], sign)
+    gz = banded(dz, profile[0], sign)
+    gx = banded(dx, profile[1], sign)
     left = (gz[:, None, :] * gx[None, :, :]).reshape(dz.shape[0] * STEP, dz.shape[1])
-    return split(left), split(banded(dy, profile[2:3], sign))
+    return split(left), split(banded(dy, profile[2], sign))
 
 
 def correlate(block, left, left_high, right_high, right_low):
@@ -77,13 +77,15 @@
         return lax.rem(value + size, size)
 
     barrier = pltpu.get_barrier_semaphore()
-    for dv in range(views):
-        for dt in (0, 1, -1):
-            if dv or dt:
-                pl.semaphore_signal(
-                    barrier, inc=1, device_id=(around(view + dv, views), around(tile + dt, tiles)),
-                    device_id_type=MESH,
-                )
+    for side in (0, 1):
+        @pl.when(tile != side * (tiles - 1))
+        def _(side=side):
+            pl.semaphore_signal(
+                barrier, inc=1, device_id=(view, tile + 2 * side - 1), device_id_type=MESH)
+
+    for dv in range(1, views):
+        pl.semaphore_signal(
+            barrier, inc=1, device_id=(around(view + dv, views), tile), device_id_type=MESH)
 
     def own_image():
         return pltpu.make_async_copy(
@@ -93,8 +95,12 @@
     def own_slab():
         return pltpu.make_async_copy(est, ext.at[0, :, pl.ds(half, rows), :], load_sem.at[1])
 
+    def own_taps():
+        return pltpu.make_async_copy(prof, prof_all.at[0], load_sem.at[2])
+
+    own_taps().start()
+    own_slab().start()
     own_image().start()
-    own_slab().start()
 
     def rim(n, side, first=False):
         here = pl.multiple_of(half * side, half)
@@ -104,7 +110,7 @@
             src_ref=source,
             dst_ref=ext.at[n, :, pl.ds(pl.multiple_of((half + rows) * (1 - side), half), half), :],
             send_sem=s_send.at[n, side], recv_sem=s_recv.at[n, side],
-            device_id=(view, around(tile + 2 * side - 1, tiles)), device_id_type=MESH)
+            device_id=(view, tile + 2 * side - 1), device_id_type=MESH)
 
     def block(n):
         to = around(view - n, views)
@@ -117,40 +123,39 @@
             send_sem=i_send.at[n, 2], recv_sem=i_recv.at[n, 2],
             device_id=(to, tile), device_id_type=MESH)
 
-    def shot_rim(n, side):
-        to, planes = block(n)
-        here = pl.multiple_of((rows - STEP) * side, STEP)
+    def shot_rim(n, side, first=False):
+        here = (rows - STEP) * side
         there = pl.multiple_of((rows + STEP) * (1 - side), STEP)
-        return pltpu.make_async_remote_copy(
-            src_ref=img.at[planes, pl.ds(here, STEP), :],
+        source = img.at[block(0)[1], pl.ds(pl.multiple_of(here, STEP), STEP), :] if first else shots.at[
+            n, :, pl.ds(pl.multiple_of(STEP + here, STEP), STEP), :]
+        return pltpu.make_async_remote_copy(
+            src_ref=source,
             dst_ref=shots.at[n, :, pl.ds(there, STEP), :],
             send_sem=i_send.at[n, side], recv_sem=i_recv.at[n, side],
-            device_id=(to, around(tile + 2 * side - 1, tiles)), device_id_type=MESH)
+            device_id=(view, tile + 2 * side - 1), device_id_type=MESH)
 
     def taps(n):
         return pltpu.make_async_remote_copy(
             src_ref=prof, dst_ref=prof_all.at[n], send_sem=p_send.at[n], recv_sem=p_recv.at[n],
             device_id=(around(view - n, views), tile), device_id_type=MESH)
 
-    def send_shots(n):
-        shot(n).start()
-        shot_rim(n, 0).start()
-        shot_rim(n, 1).start()
-
-    prof_all[0] = prof[...]
     dz, dx, dy = offsets(depth, width)
-    pl.semaphore_wait(barrier, 3 * views - 1)
+    at_end = (tile == 0).astype(jnp.int32) + (tile == tiles - 1).astype(jnp.int32)
+    pl.semaphore_wait(barrier, views + 1 - at_end)
 
     for side in (0, 1):
-        rim(0, side, True).start()
-    for side in (0, 1):
-        shot_rim(0, side).start()
+        @pl.when(tile != side * (tiles - 1))
+        def _(side=side):
+            rim(0, side, True).start()
+            shot_rim(0, side, True).start()
+
     for n in range(1, views):
         taps(n).start()
     for n in range(1, AHEAD):
-        send_shots(n)
+        shot(n).start()
+    own_taps().wait()
+    own_slab().wait()
     own_image().wait()
-    own_slab().wait()
 
     def forward(n, start):
         got = correlate(ext[n, :, pl.ds(start, rows), :], zx[0], zx[0, :wide], yy[0, 0], yy[0, 1])
@@ -161,7 +166,7 @@
     def update(n, carry):
         @pl.when(n + AHEAD < views)
         def _():
-            send_shots(n + AHEAD)
+            shot(n + AHEAD).start()
 
         @pl.when(n > 0)
         def _():
@@ -175,10 +180,6 @@
             yy[which, 0] = right[0]
             yy[which, 1] = right[1]
 
-        @pl.when(n > 0)
-        def _():
-            shot(n).wait_recv()
-
         inner = forward(n, half)
         for i in (0, 1):
             quot[:, half + i * STEP : half + (i + 1) * STEP, :] = inner[i]
@@ -187,8 +188,19 @@
             side = number * odd + (1 - number) * (1 - odd)
             edge = tile == side * (tiles - 1)
             start = pl.multiple_of(side * rows, rows)
-            rim(n, 1 - side).wait_recv()
-            shot_rim(n, 1 - side).wait_recv()
+
+            @pl.when(jnp.logical_and(number == 1, n < views - 1))
+            def _():
+                shot(n + 1).wait_recv()
+                for other in (0, 1):
+                    @pl.when(tile != other * (tiles - 1))
+                    def _(other=other):
+                        shot_rim(n + 1, other).start()
+
+            @pl.when(jnp.logical_not(edge))
+            def _():
+                rim(n, 1 - side).wait_recv()
+                shot_rim(n, 1 - side).wait_recv()
 
             @pl.when(edge)
             def _():
@@ -205,7 +217,7 @@
                 place = pl.ds(pl.multiple_of(half + begin + i * STEP, STEP), STEP)
                 ext[n + 1, :, place, :] = ext[n, :, place, :] * got[i]
 
-            @pl.when(n < views - 1)
+            @pl.when(jnp.logical_and(n < views - 1, jnp.logical_not(edge)))
             def _():
                 rim(n + 1, side).start()
 
@@ -218,8 +230,10 @@
 
     def drain(n, carry):
         for side in (0, 1):
-            rim(n, side).wait_send()
-            shot_rim(n, side).wait_send()
+            @pl.when(tile != side * (tiles - 1))
+            def _(side=side):
+                rim(n, side).wait_send()
+                shot_rim(n, side).wait_send()
 
         @pl.when(n > 0)
         def _():
@@ -233,21 +247,20 @@
 
 def shards(views, tiles, estimate, images, profiles):
     depth, rows, width = estimate.shape
-    profile = jnp.pad(profiles[0], ((0, 5), (0, width - TAPS)))
-    anywhere, vmem = (pl.BlockSpec(memory_space=space) for space in (pl.ANY, pltpu.VMEM))
+    far, near = (pl.BlockSpec(memory_space=space) for space in (pltpu.HBM, pltpu.VMEM))
     return pl.pallas_call(
         functools.partial(kernel, views, tiles),
         out_shape=jax.ShapeDtypeStruct(estimate.shape, estimate.dtype),
-        in_specs=[anywhere, anywhere, vmem],
-        out_specs=vmem,
+        in_specs=[far, far, far],
+        out_specs=near,
         scratch_shapes=[
             pltpu.VMEM((views + 1, depth, 2 * rows, width), jnp.float32),
             pltpu.VMEM((views, depth, rows + 2 * STEP, width), jnp.float32),
             pltpu.VMEM((depth, rows + 2 * STEP, width), jnp.float32),
-            pltpu.VMEM((views, 8, width), jnp.float32),
+            pltpu.VMEM((views, 3, 1, TAPS), jnp.float32),
             pltpu.VMEM((2, 2 * depth * STEP, depth * WIDE), jnp.bfloat16),
             pltpu.VMEM((2, 2, width, width), jnp.bfloat16),
-            pltpu.SemaphoreType.DMA((2,)),
+            pltpu.SemaphoreType.DMA((3,)),
             pltpu.SemaphoreType.DMA((views, 2)),
             pltpu.SemaphoreType.DMA((views, 2)),
             pltpu.SemaphoreType.DMA((views, 3)),
@@ -256,8 +269,8 @@
             pltpu.SemaphoreType.DMA((views,)),
         ],
         compiler_params=pltpu.CompilerParams(
-            collective_id=0, has_side_effects=True, vmem_limit_bytes=48 << 20),
-    )(estimate, images[0], profile)
+            collective_id=0, has_side_effects=True, vmem_limit_bytes=64000000),
+    )(estimate, images[0], jnp.transpose(profiles, (1, 0, 2)))
 
 
 def solution(mesh):

time: 81.3 us -> 69.9 us (0.86)
  Pallas kernels: 77.2 us -> 68.1 us
  local copies, waits for them, and re-layouts: 3.93 us -> 1.67 us
    pallas_call x1, Pallas kernels: 77.2 us -> 68.1 us  [shards(): pl.pallas_call(functools.partial(kernel, views, tiles), out_shape=jax.Sha...]
    unnamed x6 -> x1, local copies, waits for them, and re-layouts: 3.93 us -> 1.67 us
where the time goes in v2:
time: 69.9 us; the launch traced here: 69.8 us
  Pallas kernels  68.1 us (97%)
  local copies, waits for them, and re-layouts  1.67 us (2%)
    pallas_call x1, Pallas kernels, shards(): pl.pallas_call(functools.partial(kernel, views, tiles), out_shape=jax.Sha...  68.1 us
    unnamed x1, local copies, waits for them, and re-layouts  1.67 us

profile of v2, /device:TPU:6, one launch (start us, length us, event | category | flops | bytes accessed | tf_op | source)
XLA Modules:
  0.0 69.8 jit_solution(14084135166447938743)
XLA Ops:
  0.0 68.1 %shard_map.37 = f32[16,32,128]{2,1,0:T(8,128)} custom-call(f32[16,32,128]{2,1,0:T(8,128)} %est.1, f32[128,32,128]{2,1,0:T(8,128)} %bitcast.2, f32[3,1,15]{2,1,0:T(1,128)} %bitcast.3), custom_call_target="tpu_custom_call" | custom-call | tf_op jit(solution)/shard_map/pallas_call | solution.py:251
  68.1 1.7 %copy.5 = f32[16,32,128]{2,1,0:T(8,128)} copy(f32[16,32,128]{2,1,0:T(8,128)} %shard_map.37) | data formatting | bytes 524288

commit v3 on v2

v3 whole, which is shorter than its diff:
```python
import functools

import jax
import jax.numpy as jnp
from jax import lax
from jax.experimental import pallas as pl
from jax.experimental.pallas import tpu as pltpu
from jax.sharding import PartitionSpec as P

MESH = pl.DeviceIdType.MESH
TAPS = 15
RADIUS = 7
STEP = 8
WIDE = 3 * STEP
AHEAD = 4


def split(value):
    high = value.astype(jnp.bfloat16)
    low = (value - high.astype(jnp.float32)).astype(jnp.bfloat16)
    return high, low


def dot(a, b):
    return jnp.dot(a, b, preferred_element_type=jnp.float32)


def offsets(depth, width):
    lanes = depth * WIDE
    column = lax.broadcasted_iota(jnp.int32, (depth, lanes), 1)
    plane = (column * 2731) >> 16
    dz = plane - lax.broadcasted_iota(jnp.int32, (depth, lanes), 0)
    column = lax.broadcasted_iota(jnp.int32, (STEP, lanes), 1)
    row = column - ((column * 2731) >> 16) * WIDE
    dx = row - lax.broadcasted_iota(jnp.int32, (STEP, lanes), 0) - STEP
    dy = lax.broadcasted_iota(jnp.int32, (width, width), 0) - lax.broadcasted_iota(
        jnp.int32, (width, width), 1
    )
    return dz, dx, dy


def banded(difference, taps, sign):
    result = jnp.zeros(difference.shape, jnp.float32)
    for k in range(TAPS):
        result = jnp.where(difference == sign * (k - RADIUS), taps[:, k : k + 1], result)
    return result


def matrices(profile, dz, dx, dy, sign):
    gz = banded(dz, profile[0], sign)
    gx = banded(dx, profile[1], sign)
    left = (gz[:, None, :] * gx[None, :, :]).reshape(dz.shape[0] * STEP, dz.shape[1])
    return split(left), split(banded(dy, profile[2], sign))


def correlate(block, left, left_high, right_high, right_low):
    depth, _, width = block.shape
    rows = depth * STEP
    flat = [block[:, i * STEP : i * STEP + WIDE, :].reshape(depth * WIDE, width) for i in (0, 1)]
    high, low = split(jnp.concatenate(flat, axis=1))
    both = dot(left, high)
    mid = both[:rows] + (both[rows:] + dot(left_high, low))
    mid = jnp.concatenate([mid[:, :width], mid[:, width:]], axis=0)
    high, low = split(mid)
    out = dot(high, right_high) + (dot(low, right_high) + dot(high, right_low))
    return [out[i * rows : (i + 1) * rows].reshape(depth, STEP, width) for i in (0, 1)]


def kernel(views, tiles, est, img, prof, out, ext, shots, quot, middle, prof_all, zx, yy,
           load_sem, s_send, s_recv, i_send, i_recv, p_send, p_recv):
    view, tile = lax.axis_index("view"), lax.axis_index("tile")
    depth, rows, width = est.shape
    half = rows // 2
    wide = depth * STEP
    skirt = 3 * STEP

    def around(value, size):
        return lax.rem(value + size, size)

    def inside(side):
        return tile != side * (tiles - 1)

    def at(row, size=STEP):
        return pl.ds(pl.multiple_of(row, STEP), size)

    barrier = pltpu.get_barrier_semaphore()
    for side in (0, 1):
        @pl.when(inside(side))
        def _(side=side):
            pl.semaphore_signal(
                barrier, inc=1, device_id=(view, tile + 2 * side - 1), device_id_type=MESH)

    for dv in range(1, views):
        pl.semaphore_signal(
            barrier, inc=1, device_id=(around(view + dv, views), tile), device_id_type=MESH)

    def block(n):
        to = around(view - n, views)
        return to, pl.ds(pl.multiple_of(to * depth, depth), depth)

    own = [
        pltpu.make_async_copy(prof, prof_all.at[0], load_sem.at[0]),
        pltpu.make_async_copy(est, ext.at[0, :, pl.ds(rows, rows), :], load_sem.at[1]),
        pltpu.make_async_copy(
            img.at[block(0)[1]], shots.at[0, :, pl.ds(skirt, rows), :], load_sem.at[2]),
    ]
    for copy in own:
        copy.start()

    def rim(m, side, part, first=False):
        here = pl.ds(half * part, half)
        source = est.at[:, here, :] if first else ext.at[m, :, pl.ds(rows + half * part, half), :]
        return pltpu.make_async_remote_copy(
            src_ref=source,
            dst_ref=ext.at[m, :, at(2 * rows * (1 - side) + half * part, half), :],
            send_sem=s_send.at[m, side, part], recv_sem=s_recv.at[m, side, part],
            device_id=(view, tile + 2 * side - 1), device_id_type=MESH)

    def shot(n):
        to, planes = block(n)
        return pltpu.make_async_remote_copy(
            src_ref=img.at[planes], dst_ref=shots.at[n, :, pl.ds(skirt, rows), :],
            send_sem=i_send.at[n, 2], recv_sem=i_recv.at[n, 2],
            device_id=(to, tile), device_id_type=MESH)

    def shot_rim(m, second, side, first=False):
        n = 2 * m + second
        size = STEP if second else skirt
        here = (rows - size) * side
        there = (skirt + rows) * (1 - side) + (skirt - size) * side
        source = img.at[block(0)[1], at(here, size), :] if first else shots.at[
            n, :, at(skirt + here, size), :]
        return pltpu.make_async_remote_copy(
            src_ref=source, dst_ref=shots.at[n, :, at(there, size), :],
            send_sem=i_send.at[n, side], recv_sem=i_recv.at[n, side],
            device_id=(view, tile + 2 * side - 1), device_id_type=MESH)

    def taps(n):
        return pltpu.make_async_remote_copy(
            src_ref=prof, dst_ref=prof_all.at[n], send_sem=p_send.at[n], recv_sem=p_recv.at[n],
            device_id=(around(view - n, views), tile), device_id_type=MESH)

    def pass_on(m, second):
        shot(2 * m + second).wait_recv()
        for side in (0, 1):
            @pl.when(inside(side))
            def _(side=side):
                shot_rim(m, second, side).start()

    dz, dx, dy = offsets(depth, width)
    at_end = (tile == 0).astype(jnp.int32) + (tile == tiles - 1).astype(jnp.int32)
    pl.semaphore_wait(barrier, views + 1 - at_end)

    for side in (0, 1):
        @pl.when(inside(side))
        def _(side=side):
            for part in (1 - side, side):
                rim(0, side, part, True).start()
            shot_rim(0, 0, side, True).start()

    for n in range(1, views):
        taps(n).start()
    for n in range(1, AHEAD):
        shot(n).start()
    for copy in own:
        copy.wait()

    def product(window, second, back):
        return correlate(window, zx[second, back], zx[second, back, :wide],
                         yy[second, back, 0], yy[second, back, 1])

    def quotient(m, second, i, edge):
        if second:
            got = product(middle[:, at(STEP * (i + 1), rows), :], 1, 0)
        else:
            got = product(ext[m, :, at(STEP * (i + 3), rows), :], 0, 0)
        for k in (0, 1):
            value = shots[2 * m + second, :, at(STEP * (i + k) + skirt), :] / got[k]
            if edge is not None:
                beyond = jnp.logical_or(i + k < 0, i + k >= rows // STEP)
                value = jnp.where(jnp.logical_and(edge, beyond), 0.0, value)
            got[k] = value
        return got

    def keep(second, i, values):
        for k in (0, 1):
            quot[second, :, at(STEP * (i + k + (1 if second else 3))), :] = values[k]

    def pair(m, carry):
        @pl.when(2 * m + AHEAD < views)
        def _():
            shot(2 * m + AHEAD).start()

        @pl.when(2 * m + AHEAD + 1 < views)
        def _():
            shot(2 * m + AHEAD + 1).start()

        for second in (0, 1):
            n = 2 * m + second
            if second:
                taps(n).wait_recv()
            else:
                @pl.when(m > 0)
                def _():
                    taps(n).wait_recv()
            for which, sign in ((0, 1), (1, -1)):
                left, right = matrices(prof_all[n], dz, dx, dy, sign)
                zx[second, which, :wide] = left[0]
                zx[second, which, wide:] = left[1]
                yy[second, which, 0] = right[0]
                yy[second, which, 1] = right[1]

        @pl.when(m > 0)
        def _():
            pass_on(m, 0)

        keep(0, 1, quotient(m, 0, 1, None))
        pass_on(m, 1)

        def one_side(number, carry):
            odd = lax.rem(tile, 2)
            side = number * odd + (1 - number) * (1 - odd)
            edge = tile == side * (tiles - 1)

            @pl.when(jnp.logical_not(edge))
            def _():
                for part in (0, 1):
                    rim(m, 1 - side, part).wait_recv()
                shot_rim(m, 0, 1 - side).wait_recv()

            @pl.when(edge)
            def _():
                ext[m, :, at(2 * rows * side, rows), :] = jnp.zeros((depth, rows, width), jnp.float32)

            starts = [6 * side - 3, 6 * side - 1]
            for i, values in zip(starts, [quotient(m, 0, i, edge) for i in starts]):
                keep(0, i, values)

            starts = [4 * side - 2, 4 * side]
            found = [product(quot[0, :, at(STEP * (i + 2), rows), :], 0, 1) for i in starts]
            for i, got in zip(starts, found):
                for k in (0, 1):
                    middle[:, at(STEP * (i + k + 2)), :] = (
                        ext[m, :, at(STEP * (i + k + 4)), :] * got[k])

            @pl.when(jnp.logical_not(edge))
            def _():
                shot_rim(m, 1, 1 - side).wait_recv()

            keep(1, 4 * side - 1, quotient(m, 1, 4 * side - 1, edge))
            return carry

        lax.fori_loop(0, 2, one_side, 0)
        keep(1, 1, quotient(m, 1, 1, None))
        found = [product(quot[1, :, pl.ds(half * part, rows), :], 1, 1) for part in (0, 1)]
        for part in (0, 1):
            got = found[part]
            for k in (0, 1):
                ext[m + 1, :, pl.ds(rows + half * part + STEP * k, STEP), :] = (
                    middle[:, pl.ds(half + half * part + STEP * k, STEP), :] * got[k])
            for side in (0, 1):
                @pl.when(jnp.logical_and(m < views // 2 - 1, inside(side)))
                def _(side=side, part=part):
                    rim(m + 1, side, part).start()
        return carry

    lax.fori_loop(0, views // 2, pair, 0)
    result = pltpu.make_async_copy(ext.at[views // 2, :, pl.ds(rows, rows), :], out, load_sem.at[1])
    result.start()

    def drain(m, carry):
        for side in (0, 1):
            @pl.when(inside(side))
            def _(side=side):
                for k in (0, 1):
                    rim(m, side, k).wait_send()
                    shot_rim(m, k, side).wait_send()

        for second in (0, 1):
            @pl.when(2 * m + second > 0)
            def _(second=second):
                shot(2 * m + second).wait_send()
                taps(2 * m + second).wait_send()

        return carry

    lax.fori_loop(0, views // 2, drain, 0)
    result.wait()


def shards(views, tiles, estimate, images, profiles):
    depth, rows, width = estimate.shape
    far = pl.BlockSpec(memory_space=pltpu.HBM)
    return pl.pallas_call(
        functools.partial(kernel, views, tiles),
        out_shape=jax.ShapeDtypeStruct(estimate.shape, estimate.dtype),
        in_specs=[far, far, far],
        out_specs=far,
        scratch_shapes=[
            pltpu.VMEM((views // 2 + 1, depth, 3 * rows, width), jnp.float32),
            pltpu.VMEM((views, depth, rows + 6 * STEP, width), jnp.float32),
            pltpu.VMEM((2, depth, rows + 6 * STEP, width), jnp.float32),
            pltpu.VMEM((depth, rows + 4 * STEP, width), jnp.float32),
            pltpu.VMEM((views, 3, 1, TAPS), jnp.float32),
            pltpu.VMEM((2, 2, 2 * depth * STEP, depth * WIDE), jnp.bfloat16),
            pltpu.VMEM((2, 2, 2, width, width), jnp.bfloat16),
            pltpu.SemaphoreType.DMA((3,)),
            pltpu.SemaphoreType.DMA((views // 2, 2, 2)),
            pltpu.SemaphoreType.DMA((views // 2, 2, 2)),
            pltpu.SemaphoreType.DMA((views, 3)),
            pltpu.SemaphoreType.DMA((views, 3)),
            pltpu.SemaphoreType.DMA((views,)),
            pltpu.SemaphoreType.DMA((views,)),
        ],
        compiler_params=pltpu.CompilerParams(
            collective_id=0, has_side_effects=True, vmem_limit_bytes=64000000),
    )(estimate, images[0], jnp.transpose(profiles, (1, 0, 2)))


def solution(mesh):
    return jax.shard_map(
        functools.partial(shards, mesh.shape["view"], mesh.shape["tile"]),
        mesh=mesh,
        in_specs=(P("view", "tile", None), P("view", None, "tile", None), P("view", None, None)),
        out_specs=P("view", "tile", None),
        check_vma=False,
    )
```

time: 69.9 us -> 67.2 us (0.961)
  Pallas kernels: 68.1 us -> 65.3 us
    pallas_call x1, Pallas kernels: 68.1 us -> 65.3 us  [shards(): pl.pallas_call(functools.partial(kernel, views, tiles), out_shape=jax.Sha...]
where the time goes in v3:
time: 67.2 us; the launch traced here: 67 us
  Pallas kernels  65.3 us (97%)
  local copies, waits for them, and re-layouts  1.67 us (2%)
    pallas_call x1, Pallas kernels, shards(): pl.pallas_call(functools.partial(kernel, views, tiles), out_shape=jax.Sha...  65.3 us
    unnamed x1, local copies, waits for them, and re-layouts  1.67 us

profile of v3, /device:TPU:6, one launch (start us, length us, event | category | flops | bytes accessed | tf_op | source)
XLA Modules:
  0.0 67.0 jit_solution(18023783537270557467)
XLA Ops:
  0.0 65.3 %shard_map.37 = f32[16,32,128]{2,1,0:T(8,128)} custom-call(f32[16,32,128]{2,1,0:T(8,128)} %est.1, f32[128,32,128]{2,1,0:T(8,128)} %bitcast.2, f32[3,1,15]{2,1,0:T(1,128)} %bitcast.3), custom_call_target="tpu_custom_call" | custom-call | tf_op jit(solution)/shard_map/pallas_call | solution.py:294
  65.4 1.7 %copy.5 = f32[16,32,128]{2,1,0:T(8,128)} copy(f32[16,32,128]{2,1,0:T(8,128)} %shard_map.37) | data formatting | bytes 524288

commit v4 on v3

--- a/solution.py
+++ b/solution.py
@@ -108,8 +108,8 @@
         copy.start()
 
     def rim(m, side, part, first=False):
-        here = pl.ds(half * part, half)
-        source = est.at[:, here, :] if first else ext.at[m, :, pl.ds(rows + half * part, half), :]
+        source = est.at[:, at(half * part, half), :] if first else ext.at[
+            m, :, at(rows + half * part, half), :]
         return pltpu.make_async_remote_copy(
             src_ref=source,
             dst_ref=ext.at[m, :, at(2 * rows * (1 - side) + half * part, half), :],
@@ -154,7 +154,7 @@
     for side in (0, 1):
         @pl.when(inside(side))
         def _(side=side):
-            for part in (1 - side, side):
+            for part in (side, 1 - side):
                 rim(0, side, part, True).start()
             shot_rim(0, 0, side, True).start()
 
@@ -165,26 +165,24 @@
     for copy in own:
         copy.wait()
 
+    odd = lax.rem(tile, 2)
+
     def product(window, second, back):
         return correlate(window, zx[second, back], zx[second, back, :wide],
                          yy[second, back, 0], yy[second, back, 1])
 
-    def quotient(m, second, i, edge):
+    def blurred(m, second, i):
         if second:
-            got = product(middle[:, at(STEP * (i + 1), rows), :], 1, 0)
-        else:
-            got = product(ext[m, :, at(STEP * (i + 3), rows), :], 0, 0)
+            return product(middle[:, at(STEP * (i + 1), rows), :], 1, 0)
+        return product(ext[m, :, at(STEP * (i + 3), rows), :], 0, 0)
+
+    def keep(m, second, i, edge, got):
         for k in (0, 1):
             value = shots[2 * m + second, :, at(STEP * (i + k) + skirt), :] / got[k]
             if edge is not None:
                 beyond = jnp.logical_or(i + k < 0, i + k >= rows // STEP)
                 value = jnp.where(jnp.logical_and(edge, beyond), 0.0, value)
-            got[k] = value
-        return got
-
-    def keep(second, i, values):
-        for k in (0, 1):
-            quot[second, :, at(STEP * (i + k + (1 if second else 3))), :] = values[k]
+            quot[second, :, at(STEP * (i + k + (1 if second else 3))), :] = value
 
     def pair(m, carry):
         @pl.when(2 * m + AHEAD < views)
@@ -214,27 +212,35 @@
         def _():
             pass_on(m, 0)
 
-        keep(0, 1, quotient(m, 0, 1, None))
+        keep(m, 0, 1, None, blurred(m, 0, 1))
         pass_on(m, 1)
 
         def one_side(number, carry):
-            odd = lax.rem(tile, 2)
             side = number * odd + (1 - number) * (1 - odd)
             edge = tile == side * (tiles - 1)
 
+            @pl.when(edge)
+            def _():
+                ext[m, :, at(2 * rows * side, rows), :] = jnp.zeros((depth, rows, width), jnp.float32)
+
             @pl.when(jnp.logical_not(edge))
             def _():
-                for part in (0, 1):
-                    rim(m, 1 - side, part).wait_recv()
+                rim(m, 1 - side, 1 - side).wait_recv()
+
+            close = blurred(m, 0, 4 * side - 1)
+
+            @pl.when(jnp.logical_not(edge))
+            def _():
+                rim(m, 1 - side, side).wait_recv()
+
+            beyond = blurred(m, 0, 8 * side - 3)
+
+            @pl.when(jnp.logical_not(edge))
+            def _():
                 shot_rim(m, 0, 1 - side).wait_recv()
 
-            @pl.when(edge)
-            def _():
-                ext[m, :, at(2 * rows * side, rows), :] = jnp.zeros((depth, rows, width), jnp.float32)
-
-            starts = [6 * side - 3, 6 * side - 1]
-            for i, values in zip(starts, [quotient(m, 0, i, edge) for i in starts]):
-                keep(0, i, values)
+            keep(m, 0, 4 * side - 1, edge, close)
+            keep(m, 0, 8 * side - 3, edge, beyond)
 
             starts = [4 * side - 2, 4 * side]
             found = [product(quot[0, :, at(STEP * (i + 2), rows), :], 0, 1) for i in starts]
@@ -247,18 +253,17 @@
             def _():
                 shot_rim(m, 1, 1 - side).wait_recv()
 
-            keep(1, 4 * side - 1, quotient(m, 1, 4 * side - 1, edge))
+            keep(m, 1, 4 * side - 1, edge, blurred(m, 1, 4 * side - 1))
             return carry
 
         lax.fori_loop(0, 2, one_side, 0)
-        keep(1, 1, quotient(m, 1, 1, None))
-        found = [product(quot[1, :, pl.ds(half * part, rows), :], 1, 1) for part in (0, 1)]
-        for part in (0, 1):
-            got = found[part]
+        keep(m, 1, 1, None, blurred(m, 1, 1))
+        for part in (odd, 1 - odd):
+            got = product(quot[1, :, at(half * part, rows), :], 1, 1)
             for k in (0, 1):
-                ext[m + 1, :, pl.ds(rows + half * part + STEP * k, STEP), :] = (
-                    middle[:, pl.ds(half + half * part + STEP * k, STEP), :] * got[k])
-            for side in (0, 1):
+                ext[m + 1, :, at(rows + half * part + STEP * k), :] = (
+                    middle[:, at(half + half * part + STEP * k), :] * got[k])
+            for side in (odd, 1 - odd):
                 @pl.when(jnp.logical_and(m < views // 2 - 1, inside(side)))
                 def _(side=side, part=part):
                     rim(m + 1, side, part).start()

time: 67.2 us -> 64.7 us (0.963)
  Pallas kernels: 65.3 us -> 62.9 us
    pallas_call x1, Pallas kernels: 65.3 us -> 62.9 us  [shards(): pl.pallas_call(functools.partial(kernel, views, tiles), out_shape=jax.Sha...]
where the time goes in v4:
time: 64.7 us; the launch traced here: 64.6 us
  Pallas kernels  62.9 us (97%)
  local copies, waits for them, and re-layouts  1.67 us (3%)
    pallas_call x1, Pallas kernels, shards(): pl.pallas_call(functools.partial(kernel, views, tiles), out_shape=jax.Sha...  62.9 us
    unnamed x1, local copies, waits for them, and re-layouts  1.67 us

profile of v4, /device:TPU:6, one launch (start us, length us, event | category | flops | bytes accessed | tf_op | source)
XLA Modules:
  0.0 64.6 jit_solution(13573157225565896027)
XLA Ops:
  0.0 62.9 %shard_map.37 = f32[16,32,128]{2,1,0:T(8,128)} custom-call(f32[16,32,128]{2,1,0:T(8,128)} %est.1, f32[128,32,128]{2,1,0:T(8,128)} %bitcast.2, f32[3,1,15]{2,1,0:T(1,128)} %bitcast.3), custom_call_target="tpu_custom_call" | custom-call | tf_op jit(solution)/shard_map/pallas_call | solution.py:299
  62.9 1.7 %copy.5 = f32[16,32,128]{2,1,0:T(8,128)} copy(f32[16,32,128]{2,1,0:T(8,128)} %shard_map.37) | data formatting | bytes 524288

commit v5 on v4

--- a/solution.py
+++ b/solution.py
@@ -123,16 +123,17 @@
             send_sem=i_send.at[n, 2], recv_sem=i_recv.at[n, 2],
             device_id=(to, tile), device_id_type=MESH)
 
-    def shot_rim(m, second, side, first=False):
+    def shot_rim(m, second, side, outer=False, first=False):
         n = 2 * m + second
-        size = STEP if second else skirt
-        here = (rows - size) * side
-        there = (skirt + rows) * (1 - side) + (skirt - size) * side
+        size = half if outer else STEP
+        here = STEP if outer else (rows - STEP) * side
+        there = (skirt + rows + STEP) * (1 - side) if outer else (
+            (skirt + rows) * (1 - side) + half * side)
         source = img.at[block(0)[1], at(here, size), :] if first else shots.at[
             n, :, at(skirt + here, size), :]
         return pltpu.make_async_remote_copy(
             src_ref=source, dst_ref=shots.at[n, :, at(there, size), :],
-            send_sem=i_send.at[n, side], recv_sem=i_recv.at[n, side],
+            send_sem=i_send.at[n, side + 3 * outer], recv_sem=i_recv.at[n, side + 3 * outer],
             device_id=(view, tile + 2 * side - 1), device_id_type=MESH)
 
     def taps(n):
@@ -146,6 +147,8 @@
             @pl.when(inside(side))
             def _(side=side):
                 shot_rim(m, second, side).start()
+                if not second:
+                    shot_rim(m, second, side, True).start()
 
     dz, dx, dy = offsets(depth, width)
     at_end = (tile == 0).astype(jnp.int32) + (tile == tiles - 1).astype(jnp.int32)
@@ -156,7 +159,8 @@
         def _(side=side):
             for part in (side, 1 - side):
                 rim(0, side, part, True).start()
-            shot_rim(0, 0, side, True).start()
+            shot_rim(0, 0, side, False, True).start()
+            shot_rim(0, 0, side, True, True).start()
 
     for n in range(1, views):
         taps(n).start()
@@ -215,58 +219,52 @@
         keep(m, 0, 1, None, blurred(m, 0, 1))
         pass_on(m, 1)
 
-        def one_side(number, carry):
-            side = number * odd + (1 - number) * (1 - odd)
-            edge = tile == side * (tiles - 1)
-
-            @pl.when(edge)
+        def arrive(side, copies):
+            @pl.when(tile != side * (tiles - 1))
+            def _():
+                for copy in copies:
+                    copy.wait_recv()
+
+        def clear(side):
+            @pl.when(tile == side * (tiles - 1))
             def _():
                 ext[m, :, at(2 * rows * side, rows), :] = jnp.zeros((depth, rows, width), jnp.float32)
 
-            @pl.when(jnp.logical_not(edge))
-            def _():
-                rim(m, 1 - side, 1 - side).wait_recv()
-
-            close = blurred(m, 0, 4 * side - 1)
-
-            @pl.when(jnp.logical_not(edge))
-            def _():
-                rim(m, 1 - side, side).wait_recv()
-
-            beyond = blurred(m, 0, 8 * side - 3)
-
-            @pl.when(jnp.logical_not(edge))
-            def _():
-                shot_rim(m, 0, 1 - side).wait_recv()
-
-            keep(m, 0, 4 * side - 1, edge, close)
-            keep(m, 0, 8 * side - 3, edge, beyond)
-
-            starts = [4 * side - 2, 4 * side]
-            found = [product(quot[0, :, at(STEP * (i + 2), rows), :], 0, 1) for i in starts]
-            for i, got in zip(starts, found):
-                for k in (0, 1):
-                    middle[:, at(STEP * (i + k + 2)), :] = (
-                        ext[m, :, at(STEP * (i + k + 4)), :] * got[k])
-
-            @pl.when(jnp.logical_not(edge))
-            def _():
-                shot_rim(m, 1, 1 - side).wait_recv()
-
-            keep(m, 1, 4 * side - 1, edge, blurred(m, 1, 4 * side - 1))
-            return carry
-
-        lax.fori_loop(0, 2, one_side, 0)
-        keep(m, 1, 1, None, blurred(m, 1, 1))
-        for part in (odd, 1 - odd):
+        def first_slab(i):
+            got = product(quot[0, :, at(STEP * (i + 2), rows), :], 0, 1)
+            for k in (0, 1):
+                middle[:, at(STEP * (i + k + 2)), :] = ext[m, :, at(STEP * (i + k + 4)), :] * got[k]
+
+        def second_slab(part):
             got = product(quot[1, :, at(half * part, rows), :], 1, 1)
             for k in (0, 1):
                 ext[m + 1, :, at(rows + half * part + STEP * k), :] = (
                     middle[:, at(half + half * part + STEP * k), :] * got[k])
             for side in (odd, 1 - odd):
                 @pl.when(jnp.logical_and(m < views // 2 - 1, inside(side)))
-                def _(side=side, part=part):
+                def _(side=side):
                     rim(m + 1, side, part).start()
+
+        for side, waves in ((1 - odd, False), (odd, True)):
+            edge = tile == side * (tiles - 1)
+            clear(side)
+            arrive(side, [rim(m, 1 - side, 1 - side)])
+            got = blurred(m, 0, 4 * side - 1)
+            arrive(side, [shot_rim(m, 0, 1 - side)])
+            keep(m, 0, 4 * side - 1, edge, got)
+            first_slab(2 * side)
+            if waves:
+                keep(m, 1, 1, None, blurred(m, 1, 1))
+                second_slab(1 - side)
+            arrive(side, [rim(m, 1 - side, side)])
+            got = blurred(m, 0, 8 * side - 3)
+            arrive(side, [shot_rim(m, 0, 1 - side, True)])
+            keep(m, 0, 8 * side - 3, edge, got)
+            first_slab(6 * side - 2)
+            arrive(side, [shot_rim(m, 1, 1 - side)])
+            keep(m, 1, 4 * side - 1, edge, blurred(m, 1, 4 * side - 1))
+            if waves:
+                second_slab(side)
         return carry
 
     lax.fori_loop(0, views // 2, pair, 0)
@@ -280,6 +278,7 @@
                 for k in (0, 1):
                     rim(m, side, k).wait_send()
                     shot_rim(m, k, side).wait_send()
+                shot_rim(m, 0, side, True).wait_send()
 
         for second in (0, 1):
             @pl.when(2 * m + second > 0)
@@ -312,8 +311,8 @@
             pltpu.SemaphoreType.DMA((3,)),
             pltpu.SemaphoreType.DMA((views // 2, 2, 2)),
             pltpu.SemaphoreType.DMA((views // 2, 2, 2)),
-            pltpu.SemaphoreType.DMA((views, 3)),
-            pltpu.SemaphoreType.DMA((views, 3)),
+            pltpu.SemaphoreType.DMA((views, 5)),
+            pltpu.SemaphoreType.DMA((views, 5)),
             pltpu.SemaphoreType.DMA((views,)),
             pltpu.SemaphoreType.DMA((views,)),
         ],

time: 64.7 us -> 67.9 us (1.049)
  the two profiles are of different devices: /device:TPU:6 before, /device:TPU:3 now
where the time goes in v5:
time: 67.9 us; the launch traced here: 67.8 us
  Pallas kernels  66.1 us (97%)
  local copies, waits for them, and re-layouts  1.67 us (2%)
    pallas_call x1, Pallas kernels, shards(): pl.pallas_call(functools.partial(kernel, views, tiles), out_shape=jax.Sha...  66.1 us
    unnamed x1, local copies, waits for them, and re-layouts  1.67 us

profile of v5, /device:TPU:3, one launch (start us, length us, event | category | flops | bytes accessed | tf_op | source)
XLA Modules:
  0.0 67.8 jit_solution(9134792961976541424)
XLA Ops:
  0.0 66.1 %shard_map.37 = f32[16,32,128]{2,1,0:T(8,128)} custom-call(f32[16,32,128]{2,1,0:T(8,128)} %est.1, f32[128,32,128]{2,1,0:T(8,128)} %bitcast.2, f32[3,1,15]{2,1,0:T(1,128)} %bitcast.3), custom_call_target="tpu_custom_call" | custom-call | tf_op jit(solution)/shard_map/pallas_call | solution.py:298
  66.1 1.7 %copy.5 = f32[16,32,128]{2,1,0:T(8,128)} copy(f32[16,32,128]{2,1,0:T(8,128)} %shard_map.37) | data formatting | bytes 524288
